TPU v7x, 32 devices: a whole 2x2x4 slice. The times are simulated.
32 devices in a mesh: region: 8 (over y, x, core), brick: 4 (over z).
Axes of the slice: x: 2, y: 2, z: 4, core: 2. Of those that a mesh axis runs over, the one named last changes fastest.
Arguments:
- velocity: float32 [3, 128, 64, 256], P(None, 'region', 'brick'), may hold values from -6 to 6
- viscosity: float32 [128, 64, 256], P('region', 'brick'), may hold values from 0.05 to 0.5
- marker_pos: float32 [3, 131072], P(None, ('region', 'brick')), as said below
- marker_force: float32 [3, 131072], P(None, ('region', 'brick')), may hold values from -240 to 240
- slot_lists: int32 [32, 8192], P(('region', 'brick')), may hold values from 0 to 16384, as said below
Outputs:
- predicted: float32 [3, 128, 64, 256], P(None, 'region', 'brick')
Inputs may be any that keep to these rules, and one draw needn't show every extreme that they name: `slot_lists`: each row lists, in increasing order, the indices within its region group's 16384 markers of the markers whose second coordinate lies in that brick's rows, then is padded with 16384; every marker of the group stands in exactly one row, and in every region group one row is full. `marker_pos`: the first coordinate of a marker lies 2 or more cells inside its region group's slab, the third 2 or more cells from the grid's ends, and the second within the rows of the brick whose slot row lists it.
All inputs are finite; a program needn't handle non-finite values.
Results may differ from a plain program's by a relative error of at most 0.00088.
Values sent between devices are 32-bit elements; how exact they have to be, the bound alone decides.
No kernel may reach another device: no remote copies, remote signals or barrier semaphores. Data moves between devices by JAX's collectives and lax.ppermute only.
A program may use at most 192 MiB of HBM per device.

v0:
```python
import jax
import jax.numpy as jnp
from jax import lax
from jax.sharding import PartitionSpec as P


def from_behind(x, axis, by):
    peers = lax.axis_size(axis)
    pairs = [(i, i + by) for i in range(peers) if 0 <= i + by < peers]
    return lax.ppermute(x, axis, pairs)


def extended_2(block, sides, width):
    for axis, dim in sides:
        count = lax.axis_size(axis)
        forward = [(i, i + 1) for i in range(count - 1)]
        backward = [(target, source) for source, target in forward]
        low = lax.ppermute(
            lax.slice_in_dim(block, block.shape[dim] - width, None, axis=dim), axis, forward
        )
        high = lax.ppermute(lax.slice_in_dim(block, 0, width, axis=dim), axis, backward)
        block = jnp.concatenate([low, block, high], axis=dim)
    return block


def kernel_weight(dist):
    return jnp.where(jnp.abs(dist) < 2.0, 0.25 * (1.0 + jnp.cos(0.5 * jnp.pi * dist)), 0.0)


def spread_rows(pos, force, row_low, rows, col_low, cols, depth):
    count = pos.shape[1]
    block = 1024
    x_centre = (col_low + jnp.arange(cols, dtype=jnp.int32)).astype(jnp.float32) + 0.5
    y_centre = (row_low + jnp.arange(rows, dtype=jnp.int32)).astype(jnp.float32) + 0.5
    z_centre = jnp.arange(depth, dtype=jnp.int32).astype(jnp.float32) + 0.5

    def one_block(turn, total):
        start = turn * block
        pos_part = lax.dynamic_slice_in_dim(pos, start, block, 1)
        force_part = lax.dynamic_slice_in_dim(force, start, block, 1)
        weight_x = kernel_weight(x_centre[:, None] - pos_part[0][None, :])
        weight_y = kernel_weight(y_centre[:, None] - pos_part[1][None, :])
        weight_z = kernel_weight(z_centre[None, :] - pos_part[2][:, None])
        factor = (
            force_part[:, None, None, :] * weight_x[None, :, None, :] * weight_y[None, None, :, :]
        )
        factor = factor.reshape(3 * cols * rows, block).astype(jnp.bfloat16)
        return total + jnp.dot(
            factor, weight_z.astype(jnp.bfloat16), preferred_element_type=jnp.float32
        )

    empty = jnp.zeros((3 * cols * rows, depth), jnp.float32)
    total = lax.fori_loop(0, count // block, one_block, empty)
    return total.reshape(3, cols, rows, depth)


def side(array, axis, offset):
    parts = [slice(1, -1), slice(1, -1), slice(1, -1)]
    size = array.shape[array.ndim - 3 + axis]
    parts[axis] = slice(1 + offset, size - 1 + offset)
    if array.ndim == 4:
        return array[:, parts[0], parts[1], parts[2]]
    return array[parts[0], parts[1], parts[2]]


def advance(padded, force_field):
    vel = padded[:3]
    visc = padded[3]
    speed = side(vel, 0, 0)
    visc_mid = side(visc, 0, 0)
    diffusion = jnp.zeros_like(speed)
    advection = jnp.zeros_like(speed)
    for axis in range(3):
        upper = side(vel, axis, 1)
        lower = side(vel, axis, -1)
        visc_up = side(visc, axis, 1)
        visc_dn = side(visc, axis, -1)
        diffusion = (
            diffusion
            + 0.5 * (visc_mid + visc_up) * (upper - speed)
            - 0.5 * (visc_mid + visc_dn) * (speed - lower)
        )
        advection = advection + speed[axis][None] * (upper - lower) * 0.5
    return speed + 0.1 * (diffusion - advection + force_field)


def body(velocity, viscosity, marker_pos, marker_force, slot_lists):
    cols, own_rows, depth = viscosity.shape
    region = lax.axis_index("region")
    brick = lax.axis_index("brick")
    own_slots = slot_lists[0]
    row_low = brick * own_rows - 2
    rows = own_rows + 4
    blank = jnp.zeros((3, own_slots.shape[0]), jnp.float32)
    start = jnp.int32(0)
    pos_piece = lax.all_gather(marker_pos, "brick", axis=1, tiled=True)
    force_piece = lax.all_gather(marker_force, "brick", axis=1, tiled=True)
    length = pos_piece.shape[1]
    inside = ((own_slots >= start) & (own_slots < start + length))[None, :]
    local = jnp.clip(own_slots, 0, length - 1)
    pos = jnp.where(inside, jnp.take(pos_piece, local, axis=1), blank)
    force = jnp.where(inside, jnp.take(force_piece, local, axis=1), blank)
    field = spread_rows(pos, force, row_low, rows, region * cols, cols, depth)
    upper_rim = field[:, :, own_rows + 2 :, :]
    lower_rim = field[:, :, :2, :]
    from_below = from_behind(upper_rim, "brick", 1)
    from_above = from_behind(lower_rim, "brick", -1)
    centre = field[:, :, 2 : own_rows + 2, :]
    centre = centre.at[:, :, :2, :].add(from_below)
    force_field = centre.at[:, :, own_rows - 2 :, :].add(from_above)
    stacked = jnp.concatenate([velocity, viscosity[None]], axis=0)
    extended = extended_2(stacked, (("region", 1), ("brick", 2)), 1)
    padded = jnp.pad(extended, ((0, 0), (0, 0), (0, 0), (1, 1)))
    return advance(padded, force_field)


def solution(mesh):
    placed = (
        P(None, "region", "brick", None),
        P("region", "brick", None),
        P(None, ("region", "brick")),
        P(None, ("region", "brick")),
        P(("region", "brick"), None),
    )
    return jax.shard_map(
        body,
        mesh=mesh,
        in_specs=placed,
        out_specs=P(None, "region", "brick", None),
        check_vma=False,
    )
```

profile of v0, /device:TPU:19, one launch (start us, length us, event | category | flops | bytes accessed | tf_op | source)
XLA Modules:
  0.0 469.4 jit_solution(8026704652510305181)
XLA Ops:
  3.2 137.8 %all_gather.6 = f32[3,16384]{0,1:T(8,128)} all-gather(f32[3,4096]{0,1:T(8,128)S(1)} %copy.10), channel_id=1, replica_groups=mesh['region'=8,'brick'=4] {'brick'}, dimensions={1}, use_global_device_ids=true | all-gather | bytes 245760 | tf_op jit(solution)/shard_map/all_gather | solution.py:97
  141.7 138.8 %all_gather.7 = f32[3,16384]{0,1:T(8,128)} all-gather(f32[3,4096]{0,1:T(8,128)S(1)} %copy.11), channel_id=1, replica_groups=mesh['region'=8,'brick'=4] {'brick'}, dimensions={1}, use_global_device_ids=true | all-gather | bytes 245760 | tf_op jit(solution)/shard_map/all_gather | solution.py:96
  280.4 31.2 %gather_fusion = f32[8192,3]{1,0:T(8,128)} fusion(f32[3,16384]{0,1:T(8,128)} %all_gather.6, s32[8192]{0:T(1024)S(1)} %fusion.44), kind=kCustom, calls=%fused_computation.clone | custom fusion | bytes 229376 | tf_op jit(solution)/shard_map/jit(_take)/gather | solution.py:102
  311.7 31.3 %gather_fusion.1 = f32[8192,3]{1,0:T(8,128)} fusion(f32[3,16384]{0,1:T(8,128)} %all_gather.7, s32[8192]{0:T(1024)S(1)} %fusion.44), kind=kCustom, calls=%fused_computation.1.clone | custom fusion | bytes 229376 | tf_op jit(solution)/shard_map/jit(_take)/gather | solution.py:101
  342.9 8.0 %bitcast_select_fusion = (f32[3,8192]{0,1:T(8,128)}, f32[3,8192]{0,1:T(8,128)}) fusion(f32[8192,3]{1,0:T(8,128)} %gather_fusion.1, pred[8192]{0:T(1024)(128)(4,1)S(1)} %compare_and_fusion, pred[8192]{0:T(1024)(128)(4,1)S(1)} %and_reduce_fusion, f32[8192,3]{1,0:T(8,128)} %gather_fusion), kind=kLoop, calls=%fused_computation.47 | loop fusion | flops 98304 | bytes 409600 | tf_op jit(solution)/shard_map/jit(_where)/select_n | solution.py:101
  350.9 2.8 copy.12
  353.8 2.9 copy.13
  356.6 79.9 %while.16 = (s32[]{:T(128)}, f32[960,256]{1,0:T(8,128)S(1)}, f32[3,8192]{1,0:T(4,128)S(1)}, f32[3,8192]{1,0:T(4,128)S(1)}, s32[]{:T(128)}, /*index=5*/s32[]{:T(1...) while((s32[]{:T(128)}, f32[960,256]{1,0:T(8,128)S(1)}, ...), condition=%wide.region_1.3_spmd.clone, body=%wide.region_0.2_spmd.clone.sunk | while | flops 508179072 | bytes 11381301 | solution.py:53
  358.3 2.0 convert_element_type.63
  360.3 6.2 %convolution_add_fusion.2 = f32[960,256]{1,0:T(8,128)S(1)} fusion(bf16[960,1024]{1,0:T(8,128)(2,1)} %convert_element_type.63, f32[960,256]{1,0:T(8,128)S(1)} %get-tuple-element.284, f32[1024]{0:T(1024)S(1)} %bitcast.34, f32[256]{0:T(256)S(1)} %convert_add_fusion.8, pred[]{:T(512)S(6)} %compare.35), kind=kOutput, calls=%fused_computation.8.clone.1 | convolution fusion | flops 505905152 | bytes 3937281 | tf_op jit(solution)/shard_map/while/body/eval_jaxpr/dot_general | solution.py:48
  368.3 2.0 convert_element_type.63
  370.3 6.2 %convolution_add_fusion.2 = f32[960,256]{1,0:T(8,128)S(1)} fusion(bf16[960,1024]{1,0:T(8,128)(2,1)} %convert_element_type.63, f32[960,256]{1,0:T(8,128)S(1)} %get-tuple-element.284, f32[1024]{0:T(1024)S(1)} %bitcast.34, f32[256]{0:T(256)S(1)} %convert_add_fusion.8, pred[]{:T(512)S(6)} %compare.35), kind=kOutput, calls=%fused_computation.8.clone.1 | convolution fusion | flops 505905152 | bytes 3937281 | tf_op jit(solution)/shard_map/while/body/eval_jaxpr/dot_general | solution.py:48
  378.3 2.0 convert_element_type.63
  380.3 6.3 %convolution_add_fusion.2 = f32[960,256]{1,0:T(8,128)S(1)} fusion(bf16[960,1024]{1,0:T(8,128)(2,1)} %convert_element_type.63, f32[960,256]{1,0:T(8,128)S(1)} %get-tuple-element.284, f32[1024]{0:T(1024)S(1)} %bitcast.34, f32[256]{0:T(256)S(1)} %convert_add_fusion.8, pred[]{:T(512)S(6)} %compare.35), kind=kOutput, calls=%fused_computation.8.clone.1 | convolution fusion | flops 505905152 | bytes 3937281 | tf_op jit(solution)/shard_map/while/body/eval_jaxpr/dot_general | solution.py:48
  388.3 2.0 convert_element_type.63
  390.3 6.2 %convolution_add_fusion.2 = f32[960,256]{1,0:T(8,128)S(1)} fusion(bf16[960,1024]{1,0:T(8,128)(2,1)} %convert_element_type.63, f32[960,256]{1,0:T(8,128)S(1)} %get-tuple-element.284, f32[1024]{0:T(1024)S(1)} %bitcast.34, f32[256]{0:T(256)S(1)} %convert_add_fusion.8, pred[]{:T(512)S(6)} %compare.35), kind=kOutput, calls=%fused_computation.8.clone.1 | convolution fusion | flops 505905152 | bytes 3937281 | tf_op jit(solution)/shard_map/while/body/eval_jaxpr/dot_general | solution.py:48
  398.3 2.0 convert_element_type.63
  400.3 6.3 %convolution_add_fusion.2 = f32[960,256]{1,0:T(8,128)S(1)} fusion(bf16[960,1024]{1,0:T(8,128)(2,1)} %convert_element_type.63, f32[960,256]{1,0:T(8,128)S(1)} %get-tuple-element.284, f32[1024]{0:T(1024)S(1)} %bitcast.34, f32[256]{0:T(256)S(1)} %convert_add_fusion.8, pred[]{:T(512)S(6)} %compare.35), kind=kOutput, calls=%fused_computation.8.clone.1 | convolution fusion | flops 505905152 | bytes 3937281 | tf_op jit(solution)/shard_map/while/body/eval_jaxpr/dot_general | solution.py:48
  408.3 2.0 convert_element_type.63
  410.3 6.3 %convolution_add_fusion.2 = f32[960,256]{1,0:T(8,128)S(1)} fusion(bf16[960,1024]{1,0:T(8,128)(2,1)} %convert_element_type.63, f32[960,256]{1,0:T(8,128)S(1)} %get-tuple-element.284, f32[1024]{0:T(1024)S(1)} %bitcast.34, f32[256]{0:T(256)S(1)} %convert_add_fusion.8, pred[]{:T(512)S(6)} %compare.35), kind=kOutput, calls=%fused_computation.8.clone.1 | convolution fusion | flops 505905152 | bytes 3937281 | tf_op jit(solution)/shard_map/while/body/eval_jaxpr/dot_general | solution.py:48
  418.3 2.0 convert_element_type.63
  420.3 6.2 %convolution_add_fusion.2 = f32[960,256]{1,0:T(8,128)S(1)} fusion(bf16[960,1024]{1,0:T(8,128)(2,1)} %convert_element_type.63, f32[960,256]{1,0:T(8,128)S(1)} %get-tuple-element.284, f32[1024]{0:T(1024)S(1)} %bitcast.34, f32[256]{0:T(256)S(1)} %convert_add_fusion.8, pred[]{:T(512)S(6)} %compare.35), kind=kOutput, calls=%fused_computation.8.clone.1 | convolution fusion | flops 505905152 | bytes 3937281 | tf_op jit(solution)/shard_map/while/body/eval_jaxpr/dot_general | solution.py:48
  428.3 2.0 convert_element_type.63
  430.3 6.3 %convolution_add_fusion.2 = f32[960,256]{1,0:T(8,128)S(1)} fusion(bf16[960,1024]{1,0:T(8,128)(2,1)} %convert_element_type.63, f32[960,256]{1,0:T(8,128)S(1)} %get-tuple-element.284, f32[1024]{0:T(1024)S(1)} %bitcast.34, f32[256]{0:T(256)S(1)} %convert_add_fusion.8, pred[]{:T(512)S(6)} %compare.35), kind=kOutput, calls=%fused_computation.8.clone.1 | convolution fusion | flops 505905152 | bytes 3937281 | tf_op jit(solution)/shard_map/while/body/eval_jaxpr/dot_general | solution.py:48
  436.8 4.9 %collective-permute-start.4 = (f32[3,16,2,256]{3,2,1,0:T(2,128)S(1)}, f32[3,16,2,256]{3,2,1,0:T(2,128)S(1)}, u32[]{:S(2)}, u32[]{:S(2)}) collective-permute-start(f32[3,16,2,256]{3,2,1,0:T(2,128)S(1)} %get-tuple-element.214), channel_id=1, source_target_pairs={{0,1},{1,2},{2,3},{4,5},{5,6},{6,7},{8,9},{9,10},{10,11},{12,13},{... | collective-permute-start | bytes 294920 | tf_op jit(solution)/shard_map/ppermute | solution.py:10
  441.7 1.9 collective-permute-start.5
  443.7 5.7 %collective-permute-start = (f32[4,1,16,256]{3,2,1,0:T(8,128)S(1)}, f32[4,1,16,256]{3,2,1,0:T(8,128)S(1)}, u32[]{:S(2)}, u32[]{:S(2)}) collective-permute-start(f32[4,1,16,256]{3,2,1,0:T(8,128)S(1)} %get-tuple-element.215), channel_id=1, source_target_pairs={{0,4},{4,8},{8,12},{12,16},{16,20},{20,24},{24,28},{1,5},{5,9},{9,... | collective-permute-start | bytes 196616 | tf_op jit(solution)/shard_map/ppermute | solution.py:18
  451.4 4.4 collective-permute-done.1
  455.9 3.6 collective-permute-start.2
  459.6 2.1 collective-permute-start.3
  461.9 2.7 collective-permute-done.3
  466.6 2.8 multiply_add_fusion
  (133 shorter events, 21.5 us)
Async XLA Ops:
  3.2 137.8 %copy-start.4 = (f32[3,4096]{1,0:T(4,128)S(1)}, f32[3,4096]{1,0:T(4,128)}, u32[]{:S(2)}) copy-start(f32[3,4096]{1,0:T(4,128)} %param.15) | copy-start | bytes 147460
  356.6 0.7 copy-start.2
  360.3 6.3 %copy-start.3 = (f32[3,8192]{1,0:T(4,128)S(1)}, f32[3,8192]{1,0:T(4,128)}, u32[]{:S(2)}) copy-start(f32[3,8192]{1,0:T(4,128)} %copy-done.2) | copy-start | bytes 294916 | tf_op jit(solution)/shard_map/while
  366.6 0.7 copy-start.2
  370.3 6.3 %copy-start.3 = (f32[3,8192]{1,0:T(4,128)S(1)}, f32[3,8192]{1,0:T(4,128)}, u32[]{:S(2)}) copy-start(f32[3,8192]{1,0:T(4,128)} %copy-done.2) | copy-start | bytes 294916 | tf_op jit(solution)/shard_map/while
  376.6 0.7 copy-start.2
  380.3 6.3 %copy-start.3 = (f32[3,8192]{1,0:T(4,128)S(1)}, f32[3,8192]{1,0:T(4,128)}, u32[]{:S(2)}) copy-start(f32[3,8192]{1,0:T(4,128)} %copy-done.2) | copy-start | bytes 294916 | tf_op jit(solution)/shard_map/while
  386.6 0.7 copy-start.2
  390.3 6.3 %copy-start.3 = (f32[3,8192]{1,0:T(4,128)S(1)}, f32[3,8192]{1,0:T(4,128)}, u32[]{:S(2)}) copy-start(f32[3,8192]{1,0:T(4,128)} %copy-done.2) | copy-start | bytes 294916 | tf_op jit(solution)/shard_map/while
  396.6 0.7 copy-start.2
  400.3 6.3 %copy-start.3 = (f32[3,8192]{1,0:T(4,128)S(1)}, f32[3,8192]{1,0:T(4,128)}, u32[]{:S(2)}) copy-start(f32[3,8192]{1,0:T(4,128)} %copy-done.2) | copy-start | bytes 294916 | tf_op jit(solution)/shard_map/while
  406.6 0.7 copy-start.2
  410.3 6.3 %copy-start.3 = (f32[3,8192]{1,0:T(4,128)S(1)}, f32[3,8192]{1,0:T(4,128)}, u32[]{:S(2)}) copy-start(f32[3,8192]{1,0:T(4,128)} %copy-done.2) | copy-start | bytes 294916 | tf_op jit(solution)/shard_map/while
  416.6 0.7 copy-start.2
  420.3 6.3 %copy-start.3 = (f32[3,8192]{1,0:T(4,128)S(1)}, f32[3,8192]{1,0:T(4,128)}, u32[]{:S(2)}) copy-start(f32[3,8192]{1,0:T(4,128)} %copy-done.2) | copy-start | bytes 294916 | tf_op jit(solution)/shard_map/while
  426.6 0.7 copy-start.2
  430.3 6.3 %copy-start.3 = (f32[3,8192]{1,0:T(4,128)S(1)}, f32[3,8192]{1,0:T(4,128)}, u32[]{:S(2)}) copy-start(f32[3,8192]{1,0:T(4,128)} %copy-done.2) | copy-start | bytes 294916 | tf_op jit(solution)/shard_map/while
  436.6 7.1 %copy-start = (f32[3,16,16,256]{3,2,1,0:T(8,128)S(1)}, f32[3,16,16,256]{3,2,1,0:T(8,128)}, u32[]{:S(2)}) copy-start(f32[3,16,16,256]{3,2,1,0:T(8,128)} %param.13) | copy-start | bytes 2359300
  436.6 7.1 %copy-start.1 = (f32[16,16,256]{2,1,0:T(8,128)S(1)}, f32[16,16,256]{2,1,0:T(8,128)}, u32[]{:S(2)}) copy-start(f32[16,16,256]{2,1,0:T(8,128)} %param.14) | copy-start | bytes 786436
  436.8 24.9 %collective-permute-start.4 = (f32[3,16,2,256]{3,2,1,0:T(2,128)S(1)}, f32[3,16,2,256]{3,2,1,0:T(2,128)S(1)}, u32[]{:S(2)}, u32[]{:S(2)}) collective-permute-start(f32[3,16,2,256]{3,2,1,0:T(2,128)S(1)} %get-tuple-element.214), channel_id=1, source_target_pairs={{0,1},{1,2},{2,3},{4,5},{5,6},{6,7},{8,9},{9,10},{10,11},{12,13},{... | collective-permute-start | bytes 294920 | tf_op jit(solution)/shard_map/ppermute | solution.py:10
  441.7 20.1 %collective-permute-start.5 = (f32[3,16,2,256]{3,2,1,0:T(2,128)S(1)}, f32[3,16,2,256]{3,2,1,0:T(2,128)S(1)}, u32[]{:S(2)}, u32[]{:S(2)}) collective-permute-start(f32[3,16,2,256]{3,2,1,0:T(2,128)S(1)} %get-tuple-element.213), channel_id=1, source_target_pairs={{1,0},{2,1},{3,2},{5,4},{6,5},{7,6},{9,8},{10,9},{11,10},{13,12},{... | collective-permute-start | bytes 294920 | tf_op jit(solution)/shard_map/ppermute | solution.py:10
  443.7 7.8 %collective-permute-start = (f32[4,1,16,256]{3,2,1,0:T(8,128)S(1)}, f32[4,1,16,256]{3,2,1,0:T(8,128)S(1)}, u32[]{:S(2)}, u32[]{:S(2)}) collective-permute-start(f32[4,1,16,256]{3,2,1,0:T(8,128)S(1)} %get-tuple-element.215), channel_id=1, source_target_pairs={{0,4},{4,8},{8,12},{12,16},{16,20},{20,24},{24,28},{1,5},{5,9},{9,... | collective-permute-start | bytes 196616 | tf_op jit(solution)/shard_map/ppermute | solution.py:18
  449.3 6.5 %collective-permute-start.1 = (f32[4,1,16,256]{3,2,1,0:T(8,128)S(1)}, f32[4,1,16,256]{3,2,1,0:T(8,128)S(1)}, u32[]{:S(2)}, u32[]{:S(2)}) collective-permute-start(f32[4,1,16,256]{3,2,1,0:T(8,128)S(1)} %get-tuple-element.216), channel_id=1, source_target_pairs={{4,0},{8,4},{12,8},{16,12},{20,16},{24,20},{28,24},{5,1},{9,5},{13... | collective-permute-start | bytes 196616 | tf_op jit(solution)/shard_map/ppermute | solution.py:21
  455.9 6.0 %collective-permute-start.2 = (f32[4,18,1,256]{3,2,1,0:T(1,128)S(1)}, f32[4,18,1,256]{3,2,1,0:T(1,128)S(1)}, u32[]{:S(2)}, u32[]{:S(2)}) collective-permute-start(f32[4,18,1,256]{3,2,1,0:T(1,128)S(1)} %get-tuple-element.211), channel_id=1, source_target_pairs={{0,1},{1,2},{2,3},{4,5},{5,6},{6,7},{8,9},{9,10},{10,11},{12,13},{... | collective-permute-start | bytes 221192 | tf_op jit(solution)/shard_map/ppermute | solution.py:18
  459.6 5.1 %collective-permute-start.3 = (f32[4,18,1,256]{3,2,1,0:T(1,128)S(1)}, f32[4,18,1,256]{3,2,1,0:T(1,128)S(1)}, u32[]{:S(2)}, u32[]{:S(2)}) collective-permute-start(f32[4,18,1,256]{3,2,1,0:T(1,128)S(1)} %get-tuple-element.212), channel_id=1, source_target_pairs={{1,0},{2,1},{3,2},{5,4},{6,5},{7,6},{9,8},{10,9},{11,10},{13,12},{... | collective-permute-start | bytes 221192 | tf_op jit(solution)/shard_map/ppermute | solution.py:21
where the time goes:
time: 470 us; the launch traced here: 469 us
  blocking collectives  277 us (59%)
  local copies, waits for them, and re-layouts  88.8 us (19%)
  matrix products  50 us (11%)
  other arithmetic  25.7 us (5%)
  starting transfers between devices  20.2 us (4%)
  waiting for transfers between devices  7.14 us (2%)
    all_gather x1, blocking collectives, body(): pos_piece = lax.all_gather(marker_pos, 'brick', axis=1, tiled=True)  139 us
    all_gather x1, blocking collectives, body(): force_piece = lax.all_gather(marker_force, 'brick', axis=1, tiled=True)  138 us
    dot_general x8, matrix products, one_block(): jnp.dot(factor, weight_z.astype(jnp.bfloat16), preferred_element_type=jnp...  50 us
    gather x1, local copies, waits for them, and re-layouts, body(): pos = jnp.where(inside, jnp.take(pos_piece, local, axis=1), blank)  31.3 us
    gather x1, local copies, waits for them, and re-layouts, body(): force = jnp.where(inside, jnp.take(force_piece, local, axis=1), blank)  31.2 us
    convert_element_type x8, local copies, waits for them, and re-layouts, one_block(): factor = factor.reshape(3 * cols * rows, block).astype(jnp.bfloat16)  16 us
  transfers between devices with their start and end apart: 6, of which 2 were waited for; matrix products, arithmetic and copies ran while one was open for 0% of the time, Pallas kernels for 0%

commit v1 on v0

--- a/solution.py
+++ b/solution.py
@@ -2,6 +2,18 @@
 import jax.numpy as jnp
 from jax import lax
 from jax.sharding import PartitionSpec as P
+
+
+def gather_by_bits(x, axis, dim):
+    ways, here, turn = (lax.axis_size(axis), lax.axis_index(axis), x.shape[dim])
+    line, have = (x, 1)
+    while have < ways:
+        line = jnp.concatenate(
+            [line, lax.ppermute(line, axis, [(d, (d - have) % ways) for d in range(ways)])],
+            axis=dim,
+        )
+        have = 2 * have
+    return jnp.roll(line, here * turn, axis=dim)
 
 
 def from_behind(x, axis, by):
@@ -94,7 +106,7 @@
     blank = jnp.zeros((3, own_slots.shape[0]), jnp.float32)
     start = jnp.int32(0)
     pos_piece = lax.all_gather(marker_pos, "brick", axis=1, tiled=True)
-    force_piece = lax.all_gather(marker_force, "brick", axis=1, tiled=True)
+    force_piece = gather_by_bits(marker_force, "brick", 1)
     length = pos_piece.shape[1]
     inside = ((own_slots >= start) & (own_slots < start + length))[None, :]
     local = jnp.clip(own_slots, 0, length - 1)

time: 470 us -> 354 us (0.75); the launches traced: 469 us -> 348 us
  blocking collectives: 277 us -> 141 us
  local copies, waits for them, and re-layouts: 88.8 us -> 100 us
  matrix products: 50 us -> 57.3 us
    all_gather x1 -> x0, blocking collectives: 138 us -> none  [body(): force_piece = lax.all_gather(marker_force, 'brick', axis=1, tiled=True)]
    dot_general x8, matrix products: 50 us -> 57.3 us  [one_block(): jnp.dot(factor, weight_z.astype(jnp.bfloat16), preferred_element_type=jnp...]
    ppermute x2, waiting for transfers between devices: 7.13 us -> 0.01 us  [extended_2(): lax.ppermute(lax.slice_in_dim(block, 0, width, axis=dim), axis, backward)]
    unnamed x10 -> x43, local copies, waits for them, and re-layouts: 7.83 us -> 14.6 us
  transfers between devices with their start and end apart: 6 -> 8, of which waited for: 2 -> 2; matrix products, arithmetic and copies ran while one was open for 0% -> 12% of each run, Pallas kernels for 0% -> 0%
where the time goes in v1:
time: 354 us; the launch traced here: 348 us
  blocking collectives  141 us (40%)
  local copies, waits for them, and re-layouts  100 us (28%)
  matrix products  57.3 us (16%)
  other arithmetic  27.3 us (8%)
  starting transfers between devices  16.9 us (5%)
  waiting for transfers between devices  4.8 us (1%)
    all_gather x1, blocking collectives, body(): pos_piece = lax.all_gather(marker_pos, 'brick', axis=1, tiled=True)  141 us
    dot_general x8, matrix products, one_block(): jnp.dot(factor, weight_z.astype(jnp.bfloat16), preferred_element_type=jnp...  57.3 us
    gather x1, local copies, waits for them, and re-layouts, body(): pos = jnp.where(inside, jnp.take(pos_piece, local, axis=1), blank)  31.4 us
    gather x1, local copies, waits for them, and re-layouts, body(): force = jnp.where(inside, jnp.take(force_piece, local, axis=1), blank)  31.3 us
    convert_element_type x8, local copies, waits for them, and re-layouts, one_block(): factor = factor.reshape(3 * cols * rows, block).astype(jnp.bfloat16)  15.7 us
    unnamed x43, local copies, waits for them, and re-layouts  14.6 us
    select_n x1, other arithmetic, body(): pos = jnp.where(inside, jnp.take(pos_piece, local, axis=1), blank)  8.05 us
  transfers between devices with their start and end apart: 8, of which 2 were waited for; matrix products, arithmetic and copies ran while one was open for 12% of the time, Pallas kernels for 0%

profile of v1, /device:TPU:19, one launch (start us, length us, event | category | flops | bytes accessed | tf_op | source)
XLA Modules:
  0.0 348.1 jit_solution(3303324852212898019)
XLA Ops:
  1.7 3.9 %collective-permute-start = (f32[4,1,16,256]{3,2,1,0:T(8,128)}, f32[4,1,16,256]{3,2,1,0:T(8,128)S(1)}, u32[]{:S(2)}, u32[]{:S(2)}) collective-permute-start(f32[4,1,16,256]{3,2,1,0:T(8,128)} %get-tuple-element.221), channel_id=1, source_target_pairs={{0,4},{4,8},{8,12},{12,16},{16,20},{20,24},{24,28},{1,5},{5,9},{9,... | collective-permute-start | bytes 196616 | tf_op jit(solution)/shard_map/ppermute | solution.py:30
  10.8 2.0 slice_bitcast_fusion.3
  13.5 140.8 %all_gather.3 = f32[3,16384]{0,1:T(8,128)} all-gather(f32[3,4096]{0,1:T(8,128)S(1)} %copy.21), channel_id=1, replica_groups=mesh['region'=8,'brick'=4] {'brick'}, dimensions={1}, use_global_device_ids=true | all-gather | bytes 245760 | tf_op jit(solution)/shard_map/all_gather | solution.py:108
  154.3 31.4 %gather_fusion.1 = f32[8192,3]{1,0:T(8,128)} fusion(f32[3,16384]{0,1:T(8,128)} %all_gather.3, s32[8192]{0:T(1024)S(1)} %fusion.44), kind=kCustom, calls=%fused_computation.1.clone | custom fusion | bytes 229376 | tf_op jit(solution)/shard_map/jit(_take)/gather | solution.py:113
  186.0 2.0 collective-permute-start.2
  188.0 3.3 collective-permute-start.3
  191.3 2.7 collective-permute-done.2
  198.0 5.1 %copy.24 = f32[3,16384]{0,1:T(8,128)} copy(f32[3,16384]{1,0:T(4,128)S(1)} %constant_dynamic-slice_fusion.2) | data formatting | bytes 393216
  203.1 31.3 %gather_fusion = f32[8192,3]{1,0:T(8,128)} fusion(f32[3,16384]{0,1:T(8,128)} %copy.24, s32[8192]{0:T(1024)S(1)} %copy-done.12), kind=kCustom, calls=%fused_computation.clone | custom fusion | bytes 229376 | tf_op jit(solution)/shard_map/jit(_take)/gather | solution.py:114
  234.4 8.0 %bitcast_select_fusion = (f32[3,8192]{0,1:T(8,128)}, f32[3,8192]{0,1:T(8,128)}) fusion(f32[8192,3]{1,0:T(8,128)} %gather_fusion.1, pred[8192]{0:T(1024)(128)(4,1)S(1)} %compare_and_fusion, pred[8192]{0:T(1024)(128)(4,1)S(1)} %and_reduce_fusion, f32[8192,3]{1,0:T(8,128)} %gather_fusion), kind=kLoop, calls=%fused_computation.47 | loop fusion | flops 98304 | bytes 409600 | tf_op jit(solution)/shard_map/jit(_where)/select_n | solution.py:113
  242.4 2.8 copy.22
  245.3 2.9 copy.23
  248.1 87.1 %while.16 = (s32[]{:T(128)}, f32[960,256]{1,0:T(8,128)}, f32[3,8192]{1,0:T(4,128)S(1)}, f32[3,8192]{1,0:T(4,128)S(1)}, s32[]{:T(128)}, /*index=5*/s32[]{:T(128)}...) while((s32[]{:T(128)}, f32[960,256]{1,0:T(8,128)}, ...), condition=%wide.region_1.3_spmd.clone, body=%wide.region_0.2_spmd.clone.sunk | while | flops 508179072 | bytes 12167789 | solution.py:65
  249.9 2.0 convert_element_type.63
  251.9 6.9 %convolution_add_fusion.2 = f32[960,256]{1,0:T(8,128)} fusion(bf16[960,1024]{1,0:T(8,128)(2,1)} %convert_element_type.63, f32[960,256]{1,0:T(8,128)} %get-tuple-element.290, f32[1024]{0:T(1024)S(1)} %bitcast.34, f32[256]{0:T(256)S(1)} %convert_add_fusion.8, pred[]{:T(512)S(6)} %compare.36), kind=kOutput, calls=%fused_computation.8.clone.1 | convolution fusion | flops 505905152 | bytes 3937281 | tf_op jit(solution)/shard_map/while/body/eval_jaxpr/dot_general | solution.py:60
  260.6 2.0 convert_element_type.63
  262.5 7.2 %convolution_add_fusion.2 = f32[960,256]{1,0:T(8,128)} fusion(bf16[960,1024]{1,0:T(8,128)(2,1)} %convert_element_type.63, f32[960,256]{1,0:T(8,128)} %get-tuple-element.290, f32[1024]{0:T(1024)S(1)} %bitcast.34, f32[256]{0:T(256)S(1)} %convert_add_fusion.8, pred[]{:T(512)S(6)} %compare.36), kind=kOutput, calls=%fused_computation.8.clone.1 | convolution fusion | flops 505905152 | bytes 3937281 | tf_op jit(solution)/shard_map/while/body/eval_jaxpr/dot_general | solution.py:60
  271.5 2.0 convert_element_type.63
  273.4 7.2 %convolution_add_fusion.2 = f32[960,256]{1,0:T(8,128)} fusion(bf16[960,1024]{1,0:T(8,128)(2,1)} %convert_element_type.63, f32[960,256]{1,0:T(8,128)} %get-tuple-element.290, f32[1024]{0:T(1024)S(1)} %bitcast.34, f32[256]{0:T(256)S(1)} %convert_add_fusion.8, pred[]{:T(512)S(6)} %compare.36), kind=kOutput, calls=%fused_computation.8.clone.1 | convolution fusion | flops 505905152 | bytes 3937281 | tf_op jit(solution)/shard_map/while/body/eval_jaxpr/dot_general | solution.py:60
  282.4 2.0 convert_element_type.63
  284.4 7.2 %convolution_add_fusion.2 = f32[960,256]{1,0:T(8,128)} fusion(bf16[960,1024]{1,0:T(8,128)(2,1)} %convert_element_type.63, f32[960,256]{1,0:T(8,128)} %get-tuple-element.290, f32[1024]{0:T(1024)S(1)} %bitcast.34, f32[256]{0:T(256)S(1)} %convert_add_fusion.8, pred[]{:T(512)S(6)} %compare.36), kind=kOutput, calls=%fused_computation.8.clone.1 | convolution fusion | flops 505905152 | bytes 3937281 | tf_op jit(solution)/shard_map/while/body/eval_jaxpr/dot_general | solution.py:60
  293.3 2.0 convert_element_type.63
  295.3 7.2 %convolution_add_fusion.2 = f32[960,256]{1,0:T(8,128)} fusion(bf16[960,1024]{1,0:T(8,128)(2,1)} %convert_element_type.63, f32[960,256]{1,0:T(8,128)} %get-tuple-element.290, f32[1024]{0:T(1024)S(1)} %bitcast.34, f32[256]{0:T(256)S(1)} %convert_add_fusion.8, pred[]{:T(512)S(6)} %compare.36), kind=kOutput, calls=%fused_computation.8.clone.1 | convolution fusion | flops 505905152 | bytes 3937281 | tf_op jit(solution)/shard_map/while/body/eval_jaxpr/dot_general | solution.py:60
  304.2 2.0 convert_element_type.63
  306.2 7.2 %convolution_add_fusion.2 = f32[960,256]{1,0:T(8,128)} fusion(bf16[960,1024]{1,0:T(8,128)(2,1)} %convert_element_type.63, f32[960,256]{1,0:T(8,128)} %get-tuple-element.290, f32[1024]{0:T(1024)S(1)} %bitcast.34, f32[256]{0:T(256)S(1)} %convert_add_fusion.8, pred[]{:T(512)S(6)} %compare.36), kind=kOutput, calls=%fused_computation.8.clone.1 | convolution fusion | flops 505905152 | bytes 3937281 | tf_op jit(solution)/shard_map/while/body/eval_jaxpr/dot_general | solution.py:60
  315.2 2.0 convert_element_type.63
  317.1 7.2 %convolution_add_fusion.2 = f32[960,256]{1,0:T(8,128)} fusion(bf16[960,1024]{1,0:T(8,128)(2,1)} %convert_element_type.63, f32[960,256]{1,0:T(8,128)} %get-tuple-element.290, f32[1024]{0:T(1024)S(1)} %bitcast.34, f32[256]{0:T(256)S(1)} %convert_add_fusion.8, pred[]{:T(512)S(6)} %compare.36), kind=kOutput, calls=%fused_computation.8.clone.1 | convolution fusion | flops 505905152 | bytes 3937281 | tf_op jit(solution)/shard_map/while/body/eval_jaxpr/dot_general | solution.py:60
  328.0 7.2 %convolution_add_fusion.2 = f32[960,256]{1,0:T(8,128)} fusion(bf16[960,1024]{1,0:T(8,128)(2,1)} %convert_element_type.63, f32[960,256]{1,0:T(8,128)} %get-tuple-element.290, f32[1024]{0:T(1024)S(1)} %bitcast.34, f32[256]{0:T(256)S(1)} %convert_add_fusion.8, pred[]{:T(512)S(6)} %compare.36), kind=kOutput, calls=%fused_computation.8.clone.1 | convolution fusion | flops 505905152 | bytes 3937281 | tf_op jit(solution)/shard_map/while/body/eval_jaxpr/dot_general | solution.py:60
  336.8 2.2 collective-permute-start.6
  339.5 3.4 collective-permute-start.7
  343.0 2.1 collective-permute-done.7
  345.3 2.8 multiply_add_fusion
  (204 shorter events, 29.4 us)
Async XLA Ops:
  0.0 12.8 %copy-start.20 = (f32[3,4096]{1,0:T(4,128)S(1)}, f32[3,4096]{1,0:T(4,128)}, u32[]{:S(2)}) copy-start(f32[3,4096]{1,0:T(4,128)} %param.15) | copy-start | bytes 147460
  0.0 185.7 %collective-permute-start.4 = (f32[3,4096]{1,0:T(4,128)}, f32[3,4096]{1,0:T(4,128)S(1)}, u32[]{:S(2)}, u32[]{:S(2)}) collective-permute-start(f32[3,4096]{1,0:T(4,128)} %param.16), channel_id=1, source_target_pairs={{0,3},{1,0},{2,1},{3,2},{4,7},{5,4},{6,5},{7,6},{8,11},{9,8},{10,9... | collective-permute-start | bytes 147464 | tf_op jit(solution)/shard_map/ppermute | solution.py:12
  1.7 184.2 %collective-permute-start = (f32[4,1,16,256]{3,2,1,0:T(8,128)}, f32[4,1,16,256]{3,2,1,0:T(8,128)S(1)}, u32[]{:S(2)}, u32[]{:S(2)}) collective-permute-start(f32[4,1,16,256]{3,2,1,0:T(8,128)} %get-tuple-element.221), channel_id=1, source_target_pairs={{0,4},{4,8},{8,12},{12,16},{16,20},{20,24},{24,28},{1,5},{5,9},{9,... | collective-permute-start | bytes 196616 | tf_op jit(solution)/shard_map/ppermute | solution.py:30
  5.6 180.2 %collective-permute-start.1 = (f32[4,1,16,256]{3,2,1,0:T(8,128)}, f32[4,1,16,256]{3,2,1,0:T(8,128)S(1)}, u32[]{:S(2)}, u32[]{:S(2)}) collective-permute-start(f32[4,1,16,256]{3,2,1,0:T(8,128)} %get-tuple-element.222), channel_id=1, source_target_pairs={{4,0},{8,4},{12,8},{16,12},{20,16},{24,20},{28,24},{5,1},{9,5},{13... | collective-permute-start | bytes 196616 | tf_op jit(solution)/shard_map/ppermute | solution.py:33
  9.9 144.4 %copy-start.11 = (s32[8192]{0:T(1024)}, s32[8192]{0:T(1024)S(1)}, u32[]{:S(2)}) copy-start(s32[8192]{0:T(1024)S(1)} %fusion.44) | copy-start | bytes 98308
  13.5 172.3 %copy-start.8 = (f32[3,4096]{1,0:T(4,128)S(1)}, f32[3,4096]{1,0:T(4,128)}, u32[]{:S(2)}) copy-start(f32[3,4096]{1,0:T(4,128)} %param.16) | copy-start | bytes 147460
  13.5 172.4 %copy-start = (f32[3,16,16,256]{3,2,1,0:T(8,128)S(1)}, f32[3,16,16,256]{3,2,1,0:T(8,128)}, u32[]{:S(2)}) copy-start(f32[3,16,16,256]{3,2,1,0:T(8,128)} %param.13) | copy-start | bytes 2359300
  13.5 172.4 %copy-start.4 = (f32[16,16,256]{2,1,0:T(8,128)S(1)}, f32[16,16,256]{2,1,0:T(8,128)}, u32[]{:S(2)}) copy-start(f32[16,16,256]{2,1,0:T(8,128)} %param.14) | copy-start | bytes 786436
  154.3 37.0 %copy-start.19 = (f32[3,32768]{1,0:T(4,128)S(1)}, f32[3,32768]{1,0:T(4,128)}, u32[]{:S(2)}) copy-start(f32[3,32768]{1,0:T(4,128)} %constant_dynamic-update-slice_fusion.5) | copy-start | bytes 1179652
  185.8 12.0 %collective-permute-start.5 = (f32[3,8192]{1,0:T(4,128)S(1)}, f32[3,8192]{1,0:T(4,128)S(1)}, u32[]{:S(2)}, u32[]{:S(2)}) collective-permute-start(f32[3,8192]{1,0:T(4,128)S(1)} %pad_maximum_fusion.12), channel_id=1, source_target_pairs={{0,2},{1,3},{2,0},{3,1},{4,6},{5,7},{6,4},{7,5},{8,10},{9,11},{10,... | collective-permute-start | bytes 294920 | tf_op jit(solution)/shard_map/ppermute | solution.py:12
  186.0 8.0 %collective-permute-start.2 = (f32[4,18,1,256]{3,2,1,0:T(1,128)S(1)}, f32[4,18,1,256]{3,2,1,0:T(1,128)S(1)}, u32[]{:S(2)}, u32[]{:S(2)}) collective-permute-start(f32[4,18,1,256]{3,2,1,0:T(1,128)S(1)} %get-tuple-element.217), channel_id=1, source_target_pairs={{0,1},{1,2},{2,3},{4,5},{5,6},{6,7},{8,9},{9,10},{10,11},{12,13},{... | collective-permute-start | bytes 221192 | tf_op jit(solution)/shard_map/ppermute | solution.py:30
  188.0 6.0 %collective-permute-start.3 = (f32[4,18,1,256]{3,2,1,0:T(1,128)S(1)}, f32[4,18,1,256]{3,2,1,0:T(1,128)S(1)}, u32[]{:S(2)}, u32[]{:S(2)}) collective-permute-start(f32[4,18,1,256]{3,2,1,0:T(1,128)S(1)} %get-tuple-element.218), channel_id=1, source_target_pairs={{1,0},{2,1},{3,2},{5,4},{6,5},{7,6},{9,8},{10,9},{11,10},{13,12},{... | collective-permute-start | bytes 221192 | tf_op jit(solution)/shard_map/ppermute | solution.py:33
  262.5 7.2 %copy-start.10 = (f32[3,8192]{1,0:T(4,128)S(1)}, f32[3,8192]{1,0:T(4,128)}, u32[]{:S(2)}) copy-start(f32[3,8192]{1,0:T(4,128)} %copy-done.9) | copy-start | bytes 294916 | tf_op jit(solution)/shard_map/while
  262.5 7.2 %copy-start.18 = (f32[3,8192]{1,0:T(4,128)S(1)}, f32[3,8192]{1,0:T(4,128)}, u32[]{:S(2)}) copy-start(f32[3,8192]{1,0:T(4,128)} %copy-done.17) | copy-start | bytes 294916 | tf_op jit(solution)/shard_map/while
  273.4 7.2 %copy-start.10 = (f32[3,8192]{1,0:T(4,128)S(1)}, f32[3,8192]{1,0:T(4,128)}, u32[]{:S(2)}) copy-start(f32[3,8192]{1,0:T(4,128)} %copy-done.9) | copy-start | bytes 294916 | tf_op jit(solution)/shard_map/while
  273.4 7.2 %copy-start.18 = (f32[3,8192]{1,0:T(4,128)S(1)}, f32[3,8192]{1,0:T(4,128)}, u32[]{:S(2)}) copy-start(f32[3,8192]{1,0:T(4,128)} %copy-done.17) | copy-start | bytes 294916 | tf_op jit(solution)/shard_map/while
  284.4 7.2 %copy-start.10 = (f32[3,8192]{1,0:T(4,128)S(1)}, f32[3,8192]{1,0:T(4,128)}, u32[]{:S(2)}) copy-start(f32[3,8192]{1,0:T(4,128)} %copy-done.9) | copy-start | bytes 294916 | tf_op jit(solution)/shard_map/while
  284.4 7.2 %copy-start.18 = (f32[3,8192]{1,0:T(4,128)S(1)}, f32[3,8192]{1,0:T(4,128)}, u32[]{:S(2)}) copy-start(f32[3,8192]{1,0:T(4,128)} %copy-done.17) | copy-start | bytes 294916 | tf_op jit(solution)/shard_map/while
  295.3 7.2 %copy-start.10 = (f32[3,8192]{1,0:T(4,128)S(1)}, f32[3,8192]{1,0:T(4,128)}, u32[]{:S(2)}) copy-start(f32[3,8192]{1,0:T(4,128)} %copy-done.9) | copy-start | bytes 294916 | tf_op jit(solution)/shard_map/while
  295.3 7.2 %copy-start.18 = (f32[3,8192]{1,0:T(4,128)S(1)}, f32[3,8192]{1,0:T(4,128)}, u32[]{:S(2)}) copy-start(f32[3,8192]{1,0:T(4,128)} %copy-done.17) | copy-start | bytes 294916 | tf_op jit(solution)/shard_map/while
  306.2 7.2 %copy-start.18 = (f32[3,8192]{1,0:T(4,128)S(1)}, f32[3,8192]{1,0:T(4,128)}, u32[]{:S(2)}) copy-start(f32[3,8192]{1,0:T(4,128)} %copy-done.17) | copy-start | bytes 294916 | tf_op jit(solution)/shard_map/while
  317.1 7.2 %copy-start.10 = (f32[3,8192]{1,0:T(4,128)S(1)}, f32[3,8192]{1,0:T(4,128)}, u32[]{:S(2)}) copy-start(f32[3,8192]{1,0:T(4,128)} %copy-done.9) | copy-start | bytes 294916 | tf_op jit(solution)/shard_map/while
  317.1 7.2 %copy-start.18 = (f32[3,8192]{1,0:T(4,128)S(1)}, f32[3,8192]{1,0:T(4,128)}, u32[]{:S(2)}) copy-start(f32[3,8192]{1,0:T(4,128)} %copy-done.17) | copy-start | bytes 294916 | tf_op jit(solution)/shard_map/while
  328.0 7.2 %copy-start.18 = (f32[3,8192]{1,0:T(4,128)S(1)}, f32[3,8192]{1,0:T(4,128)}, u32[]{:S(2)}) copy-start(f32[3,8192]{1,0:T(4,128)} %copy-done.17) | copy-start | bytes 294916 | tf_op jit(solution)/shard_map/while
  336.7 8.5 %copy-start.3 = (f32[4,18,18,258]{3,2,1,0:T(8,128)S(1)}, f32[4,18,18,258]{3,2,1,0:T(8,128)}, u32[]{:S(2)}) copy-start(f32[4,18,18,258]{3,2,1,0:T(8,128)} %copy-done.2) | copy-start | bytes 4012420
  336.7 8.5 %copy-start.5 = (f32[16,16,256]{2,1,0:T(8,128)S(1)}, f32[16,16,256]{2,1,0:T(8,128)}, u32[]{:S(2)}) copy-start(f32[16,16,256]{2,1,0:T(8,128)} %get-tuple-element.223) | copy-start | bytes 786436
  336.7 8.5 %copy-start.6 = (f32[16,16,256]{2,1,0:T(8,128)S(1)}, f32[16,16,256]{2,1,0:T(8,128)}, u32[]{:S(2)}) copy-start(f32[16,16,256]{2,1,0:T(8,128)} %get-tuple-element.224) | copy-start | bytes 786436
  336.7 8.5 %copy-start.7 = (f32[16,16,256]{2,1,0:T(8,128)S(1)}, f32[16,16,256]{2,1,0:T(8,128)}, u32[]{:S(2)}) copy-start(f32[16,16,256]{2,1,0:T(8,128)} %get-tuple-element.225) | copy-start | bytes 786436
  336.7 8.5 %copy-start.14 = (f32[4,18,1,256]{3,2,1,0:T(1,128)S(1)}, f32[4,18,1,256]{3,2,1,0:T(1,128)}, u32[]{:S(2)}) copy-start(f32[4,18,1,256]{3,2,1,0:T(1,128)} %copy-done.13) | copy-start | bytes 221188
  336.7 8.5 %copy-start.16 = (f32[4,18,1,256]{3,2,1,0:T(1,128)S(1)}, f32[4,18,1,256]{3,2,1,0:T(1,128)}, u32[]{:S(2)}) copy-start(f32[4,18,1,256]{3,2,1,0:T(1,128)} %copy-done.15) | copy-start | bytes 221188
  336.8 6.2 %collective-permute-start.6 = (f32[3,16,2,256]{3,2,1,0:T(2,128)S(1)}, f32[3,16,2,256]{3,2,1,0:T(2,128)S(1)}, u32[]{:S(2)}, u32[]{:S(2)}) collective-permute-start(f32[3,16,2,256]{3,2,1,0:T(2,128)S(1)} %get-tuple-element.220), channel_id=1, source_target_pairs={{0,1},{1,2},{2,3},{4,5},{5,6},{6,7},{8,9},{9,10},{10,11},{12,13},{... | collective-permute-start | bytes 294920 | tf_op jit(solution)/shard_map/ppermute | solution.py:22
  339.5 5.6 %collective-permute-start.7 = (f32[3,16,2,256]{3,2,1,0:T(2,128)S(1)}, f32[3,16,2,256]{3,2,1,0:T(2,128)S(1)}, u32[]{:S(2)}, u32[]{:S(2)}) collective-permute-start(f32[3,16,2,256]{3,2,1,0:T(2,128)S(1)} %get-tuple-element.219), channel_id=1, source_target_pairs={{1,0},{2,1},{3,2},{5,4},{6,5},{7,6},{9,8},{10,9},{11,10},{13,12},{... | collective-permute-start | bytes 294920 | tf_op jit(solution)/shard_map/ppermute | solution.py:22
  (25 other events, 56.9 us)
